TPU v7x, 32 devices: a whole 2x2x4 slice. The times are simulated.
32 devices in a mesh: sec: 2 (over core), row: 4 (over y, x), col: 4 (over z).
Axes of the slice: x: 2, y: 2, z: 4, core: 2. Of those that a mesh axis runs over, the one named last changes fastest.
Arguments:
- anc_inverse: float32 [2048, 2048], P('row', ('sec', 'col')), as said below
- panel: float32 [8192, 2048], P(('sec', 'col'), 'row'), may hold values from -0.5 to 0.5
- diag_inverse: float32 [8192, 512], P(('sec', 'col')), may hold values from -6 to 6
- widths: int32 [16], replicated, may hold values from 1 to 4, as said below
- pattern: int32 [16, 16], replicated, may hold values 0 or 1
Outputs:
- off_inverse: float32 [8192, 2048], P(('sec', 'col'), 'row')
- child_inverse: float32 [8192, 512], P(('sec', 'col'))
Inputs may be any that keep to these rules, and one draw needn't show every extreme that they name: `anc_inverse`: exactly symmetric. `widths`: both 1 and 4 occur in every draw.
All inputs are finite; a program needn't handle non-finite values.
Results may differ from a plain program's by a relative error of at most 0.0003.
Values sent between devices are 32-bit elements; how exact they have to be, the bound alone decides.
A program may use at most 128 MiB of HBM per device.

v0:
```python
import functools
import jax
import jax.numpy as jnp
from jax import lax
from jax.experimental import pallas as pl
from jax.experimental.pallas import tpu as pltpu
from jax.sharding import PartitionSpec as P

B = 128
SW = 512
CHUNKS = 8
F32 = jnp.float32
BF = jnp.bfloat16
MESH = pl.DeviceIdType.MESH
NN = (((1,), (0,)), ((), ()))
NT = (((1,), (1,)), ((), ()))


def split(value):
    high = value.astype(BF)
    return high, (value - high.astype(F32)).astype(BF)


def dot3(ah, al, bh, bl, dims):
    dot = functools.partial(lax.dot_general, dimension_numbers=dims, preferred_element_type=F32)
    return dot(ah, bh) + (dot(ah, bl) + dot(al, bh))


def factor(count):
    low = 1
    for value in range(1, count + 1):
        if count % value == 0 and value * value <= count:
            low = value
    return count // low, low


class Group:
    def __init__(self, copies):
        self.copies = copies

    def start(self):
        for one in self.copies:
            one.start()

    def wait_recv(self):
        for one in self.copies:
            one.wait_recv()

    def wait_send(self):
        for one in self.copies:
            one.wait_send()


def kernel(
    sizes,
    anc_ref, panel_ref, diag_ref, widths_ref, pattern_ref, prod_ref, upd_ref,
    anc, ah, al, ph, plo, pin, opp, oh, ol, qsend, qrecv, upack, urecv, usum, ugat,
    zs, zr, ps, pr, os_, or_, qs, qr, us, ur, gs, gr, ds,
):
    nsec, nrow, ncol, nf, ns, nb, square = sizes
    rows, width = panel_ref.shape
    pw = anc_ref.shape[1]
    per = width // pw
    slots = rows // SW
    wb = SW // B
    tri = wb * (wb + 1) // 2
    part = tri * B // nrow
    tm = 256
    sec, row, col = lax.axis_index("sec"), lax.axis_index("row"), lax.axis_index("col")
    turn = sec if square else 0
    a, b = row // nb, row % nb
    f = a + turn * (b - a)
    s = b + turn * (a - b)
    cf = nb - turn * (nb - 1)
    cs = 1 + turn * (nb - 1)

    def at(fi, si):
        return fi * cf + si * cs

    def copy(src, dst, send, recv, where):
        return pltpu.make_async_remote_copy(
            src_ref=src, dst_ref=dst, send_sem=send, recv_sem=recv, device_id=where, device_id_type=MESH
        )

    first = (sec * ncol + col) * slots
    blocks = width // B
    fill = [widths_ref[first + j] for j in range(slots)]
    load_diag = pltpu.make_async_copy(diag_ref, upd_ref, ds)

    def inside(j, i):
        return jnp.where(fill[j] > i, 1.0, 0.0).astype(F32)

    def present(j, r, c):
        return pattern_ref[first + j, r * blocks + c].astype(F32)

    def keep(src, j, slot, r):
        for i in range(wb):
            here = pl.ds(j * SW + i * B, B)
            for c in range(blocks):
                cols = pl.ds(c * B, B)
                high, low = split(src(i, cols) * (inside(j, i) * present(j, r, c)))
                ph[slot, here, cols] = high
                plo[slot, here, cols] = low

    has_left = (col > 0).astype(jnp.int32)
    has_right = (col < ncol - 1).astype(jnp.int32)
    barrier = pltpu.get_barrier_semaphore()
    for d in range(1, nrow):
        pl.semaphore_signal(barrier, inc=1, device_id={"row": (row + d) % nrow}, device_id_type=MESH)
    pl.semaphore_signal(barrier, inc=1, device_id={"sec": 1 - sec}, device_id_type=MESH)

    @pl.when(col > 0)
    def _():
        pl.semaphore_signal(barrier, inc=1, device_id={"col": col - 1}, device_id_type=MESH)

    @pl.when(col < ncol - 1)
    def _():
        pl.semaphore_signal(barrier, inc=1, device_id={"col": col + 1}, device_id_type=MESH)

    pl.semaphore_wait(barrier, nrow + has_left + has_right)

    mine = sec * ncol + col

    def piece_copy(src, p, way):
        where = ({"col": col - 1}, {"col": col + 1}, {"sec": 1 - sec})[way]
        size = src.shape[0] // CHUNKS
        return Group([
            copy(
                src.at[pl.ds(c * size, size)], anc.at[p, pl.ds(c * size, size)],
                zs.at[p, way, c], zr.at[p, c], where,
            )
            for c in range(CHUNKS)
        ])

    def opp_copy(src, d, e, k):
        return copy(
            src, opp.at[d - 1, e - 1, k], os_.at[d - 1, e - 1, k], or_.at[d - 1, e - 1, k],
            {"row": at((f + d) % nf, s)},
        )

    def pass_on(src, p):
        for d in range(1, nf):
            for e in range(1, ns):
                @pl.when(p // per == at((f + d) % nf, (s + e) % ns))
                def _():
                    opp_copy(src, d, e, p % per).start()

    def panel_copy(d, j):
        return copy(
            panel_ref.at[pl.ds(j * SW, SW)], pin.at[d - 1, j], ps.at[d - 1, j], pr.at[d - 1, j],
            {"row": at((f + d) % nf, s)},
        )

    def halves(src, p):
        high, low = split(src[...])
        ah[p] = high
        al[p] = low

    def late(p):
        return p // per == row

    def send_mine():
        pl.when(col > 0)(lambda: piece_copy(anc_ref, mine, 0).start())
        pl.when(col < ncol - 1)(lambda: piece_copy(anc_ref, mine, 1).start())
        piece_copy(anc_ref, mine, 2).start()

    @pl.when(jnp.logical_not(late(mine)))
    def _():
        send_mine()
        pass_on(anc_ref, mine)

    for j in range(slots):
        for d in range(1, nf):
            panel_copy(d, j).start()

    load_diag.start()
    halves(anc_ref, mine)
    for j in range(slots):
        keep(lambda i, cols: panel_ref[pl.ds(j * SW + i * B, B), cols], j, 0, row)

    def relay(p, way, c, onward):
        piece_copy(anc_ref, p, way).copies[c].wait_recv()
        pl.when(onward)(lambda: piece_copy(anc.at[p], p, way).copies[c].start())
        piece_copy(anc.at[p], p, 2).copies[c].start()

    def settle(p):
        pass_on(anc.at[p], p)
        halves(anc.at[p], p)

    def from_partner(p):
        piece_copy(anc_ref, p, 2).wait_recv()
        pass_on(anc.at[p], p)
        halves(anc.at[p], p)

    other = (1 - sec) * ncol + col

    def gather(phase):
        def ready(p):
            return late(p) if phase else jnp.logical_not(late(p))

        def step(t, carry):
            left = jnp.logical_and(col - t >= 0, ready(mine - t))
            right = jnp.logical_and(col + t < ncol, ready(mine + t))
            for c in range(CHUNKS):
                pl.when(left)(lambda: relay(mine - t, 1, c, col < ncol - 1))
                pl.when(right)(lambda: relay(mine + t, 0, c, col > 0))
            pl.when(left)(lambda: settle(mine - t))
            pl.when(right)(lambda: settle(mine + t))
            partners(t)
            return carry

        def partners(t):
            left = jnp.logical_and(col - t >= 0, ready(other - t))
            right = jnp.logical_and(col + t < ncol, ready(other + t))
            pl.when(left)(lambda: from_partner(other - t))
            pl.when(jnp.logical_and(right, t > 0))(lambda: from_partner(other + t))

        partners(0)
        lax.fori_loop(1, ncol, step, 0)

    gather(0)
    pl.when(late(mine))(send_mine)

    for j in range(slots):
        for d in range(1, nf):
            panel_copy(d, j).wait_recv()
            keep(lambda i, cols: pin[d - 1, j, pl.ds(i * B, B), cols], j, d, at((f + nf - d) % nf, s))
    for d in range(1, nf):
        for e in range(1, ns):
            for k in range(per):
                opp_copy(anc_ref, d, e, k).wait_recv()
                high, low = split(opp[d - 1, e - 1, k])
                oh[d - 1, e - 1, k] = high
                ol[d - 1, e - 1, k] = low

    def q_copy(e, j):
        return copy(
            qsend.at[e - 1, j], qrecv.at[e - 1, j], qs.at[e - 1, j], qr.at[e - 1, j],
            {"row": at(f, (s + e) % ns)},
        )

    for j in range(slots):
        for e in range(1, ns):
            base = at(f, (s + e) % ns) * per

            def target(i, carry):
                r = pl.multiple_of(i * tm, tm)
                rr = pl.ds(pl.multiple_of(j * SW + r, tm), tm)
                for k in range(per):
                    acc = dot3(ph[0, rr], plo[0, rr], ah[base + k], al[base + k], NN)
                    for d in range(1, nf):
                        acc += dot3(ph[d, rr], plo[d, rr], oh[d - 1, e - 1, k], ol[d - 1, e - 1, k], NN)
                    qsend[e - 1, j, pl.ds(r, tm), pl.ds(k * pw, pw)] = acc
                return carry

            lax.fori_loop(0, SW // tm, target, 0)
            q_copy(e, j).start()

    def near(i, carry):
        rr = pl.ds(pl.multiple_of(i * tm, tm), tm)
        acc = jnp.zeros((tm, width), F32)
        for d in range(1, nf):
            for k in range(per):
                p = at((f + nf - d) % nf, s) * per + k
                cols = pl.ds(k * pw, pw)
                acc += dot3(ph[d, rr, cols], plo[d, rr, cols], ah[p], al[p], NT)
        prod_ref[rr] = acc
        return carry

    lax.fori_loop(0, rows // tm, near, 0)
    gather(1)

    def own(i, carry):
        rr = pl.ds(pl.multiple_of(i * tm, tm), tm)
        for k in range(per):
            p = row * per + k
            prod_ref[rr, pl.ds(k * pw, pw)] += dot3(ph[0, rr], plo[0, rr], ah[p], al[p], NN)
        return carry

    lax.fori_loop(0, rows // tm, own, 0)

    def u_copy(j, d):
        return copy(
            upack.at[j, pl.ds(pl.multiple_of(((row + d) % nrow) * part, 8), part)],
            urecv.at[j, d - 1], us.at[j, d - 1], ur.at[j, d - 1], {"row": (row + d) % nrow},
        )

    def g_copy(j, d):
        return copy(
            usum.at[j], ugat.at[j, d - 1], gs.at[j, d - 1], gr.at[j, d - 1], {"row": (row + d) % nrow}
        )

    for j in range(slots):
        jr = pl.ds(j * SW, SW)
        for e in range(1, ns):
            q_copy(e, j).wait_recv()
            prod_ref[jr] += qrecv[e - 1, j]
        spot = 0
        for i in range(wb):
            qh, ql = split(prod_ref[pl.ds(j * SW + i * B, B)])
            rest = pl.ds(j * SW + i * B, SW - i * B)
            line = dot3(qh, ql, ph[0, rest], plo[0, rest], NT)
            for k in range(i, wb):
                upack[j, pl.ds(spot * B, B)] = line[:, (k - i) * B:(k - i + 1) * B]
                spot += 1
        for d in range(1, nrow):
            u_copy(j, d).start()

    for j in range(slots):
        for i in range(wb):
            here = pl.ds(j * SW + i * B, B)
            for c in range(blocks):
                cols = pl.ds(c * B, B)
                prod_ref[here, cols] = prod_ref[here, cols] * -(inside(j, i) * present(j, row, c))

    for j in range(slots):
        for d in range(1, nrow):
            u_copy(j, d).wait_recv()
        total = upack[j, pl.ds(pl.multiple_of(row * part, 8), part)]
        for d in range(1, nrow):
            total += urecv[j, d - 1]
        usum[j] = total
        for d in range(1, nrow):
            g_copy(j, d).start()

    load_diag.wait()
    for j in range(slots):
        for d in range(1, nrow):
            u_copy(j, d).wait_send()
        upack[j, pl.ds(pl.multiple_of(row * part, 8), part)] = usum[j]
        for d in range(1, nrow):
            g_copy(j, d).wait_recv()
            upack[j, pl.ds(pl.multiple_of(((row + nrow - d) % nrow) * part, 8), part)] = ugat[j, d - 1]
        spot = 0
        for i in range(wb):
            for k in range(i, wb):
                block = upack[j, pl.ds(spot * B, B)]
                held = inside(j, k)
                upper = (pl.ds(j * SW + i * B, B), pl.ds(k * B, B))
                upd_ref[upper] = (upd_ref[upper] + block) * held
                if k > i:
                    lower = (pl.ds(j * SW + k * B, B), pl.ds(i * B, B))
                    upd_ref[lower] = (upd_ref[lower] + block.T) * held
                spot += 1

    for j in range(slots):
        for d in range(1, nrow):
            g_copy(j, d).wait_send()
        for e in range(1, ns):
            q_copy(e, j).wait_send()
        for d in range(1, nf):
            panel_copy(d, j).wait_send()
    for d in range(1, nf):
        for e in range(1, ns):
            for k in range(per):
                opp_copy(anc_ref, d, e, k).wait_send()

    def drain(q, carry):
        p = sec * ncol + q
        pl.when(jnp.logical_and(q <= col, col < ncol - 1))(lambda: piece_copy(anc_ref, p, 1).wait_send())
        pl.when(jnp.logical_and(q >= col, col > 0))(lambda: piece_copy(anc_ref, p, 0).wait_send())
        piece_copy(anc_ref, p, 2).wait_send()
        return carry

    lax.fori_loop(0, ncol, drain, 0)


def local(sizes, anc_inverse, panel, diag_inverse, widths, pattern):
    nsec, nrow, ncol, nf, ns, nb, square = sizes
    rows, width = panel.shape
    pw = anc_inverse.shape[1]
    per = width // pw
    slots = rows // SW
    pieces = nsec * ncol
    wb = SW // B
    packed = wb * (wb + 1) // 2 * B
    part = packed // nrow
    vm = pltpu.VMEM
    dma = pltpu.SemaphoreType.DMA
    whole = pl.BlockSpec(memory_space=pltpu.VMEM)
    scalar = pl.BlockSpec(memory_space=pltpu.SMEM)
    return pl.pallas_call(
        functools.partial(kernel, sizes),
        out_shape=(jax.ShapeDtypeStruct((rows, width), F32), jax.ShapeDtypeStruct((rows, SW), F32)),
        in_specs=[whole, whole, pl.BlockSpec(memory_space=pl.ANY), scalar, scalar],
        out_specs=(whole, whole),
        scratch_shapes=[
            vm((pieces, width, pw), F32),
            vm((pieces, width, pw), BF),
            vm((pieces, width, pw), BF),
            vm((nf, rows, width), BF),
            vm((nf, rows, width), BF),
            vm((nf - 1, slots, SW, width), F32),
            vm((nf - 1, ns - 1, per, width, pw), F32),
            vm((nf - 1, ns - 1, per, width, pw), BF),
            vm((nf - 1, ns - 1, per, width, pw), BF),
            vm((ns - 1, slots, SW, width), F32),
            vm((ns - 1, slots, SW, width), F32),
            vm((slots, packed, B), F32),
            vm((slots, nrow - 1, part, B), F32),
            vm((slots, part, B), F32),
            vm((slots, nrow - 1, part, B), F32),
            dma((pieces, 3, CHUNKS)), dma((pieces, CHUNKS)),
            dma((nf - 1, slots)), dma((nf - 1, slots)),
            dma((nf - 1, ns - 1, per)), dma((nf - 1, ns - 1, per)),
            dma((ns - 1, slots)), dma((ns - 1, slots)),
            dma((slots, nrow - 1)), dma((slots, nrow - 1)),
            dma((slots, nrow - 1)), dma((slots, nrow - 1)),
            dma,
        ],
        compiler_params=pltpu.CompilerParams(
            collective_id=0, has_side_effects=True, vmem_limit_bytes=60 * 1024 * 1024
        ),
    )(anc_inverse, panel, diag_inverse, widths, pattern)


def solution(mesh):
    shape = dict(mesh.shape)
    na, nb = factor(shape["row"])
    sizes = (shape["sec"], shape["row"], shape["col"], na, nb, nb, na == nb)
    in_specs = (
        P("row", ("sec", "col")),
        P(("sec", "col"), "row"),
        P(("sec", "col"), None),
        P(),
        P(),
    )
    out_specs = (P(("sec", "col"), "row"), P(("sec", "col"), None))
    return jax.shard_map(
        functools.partial(local, sizes), mesh=mesh, in_specs=in_specs, out_specs=out_specs, check_vma=False
    )
```

profile of v0, /device:TPU:0, one launch (start us, length us, event | category | flops | bytes accessed | tf_op | source)
XLA Modules:
  0.0 111.9 jit_solution(6568552032882061422)
XLA Ops:
  0.6 106.7 %shard_map.68 = (f32[1024,512]{1,0:T(8,128)}, f32[1024,512]{1,0:T(8,128)}) custom-call(f32[512,256]{1,0:T(8,128)} %anc_ref.1, f32[1024,512]{1,0:T(8,128)} %panel_ref.1, f32[1024,512]{1,0:T(8,128)} %diag_ref.1, s32[16]{0:T(128)} %widths_ref.1, s32[16,16]{1,0:T(8,128)} %pattern_ref.1), custom_call_target="tpu_custom_call" | custom-call | tf_op jit(solution)/shard_map/pallas_call | solution.py:382
  107.4 0.0 copy-start
  107.4 3.2 %copy.9 = f32[1024,512]{1,0:T(8,128)} copy(f32[1024,512]{1,0:T(8,128)} %get-tuple-element.4) | data formatting | bytes 4194304
  110.6 0.0 copy-done
  110.6 1.3 %copy.10 = f32[1024,512]{1,0:T(8,128)} copy(f32[1024,512]{1,0:T(8,128)S(1)} %copy-done) | data formatting | bytes 4194304
Async XLA Ops:
  107.4 3.2 %copy-start = (f32[1024,512]{1,0:T(8,128)S(1)}, f32[1024,512]{1,0:T(8,128)}, u32[]{:S(2)}) copy-start(f32[1024,512]{1,0:T(8,128)} %get-tuple-element.5) | copy-start | bytes 6291460
where the time goes:
time: 114 us; the launch traced here: 112 us
  Pallas kernels  107 us (94%)
  local copies, waits for them, and re-layouts  4.55 us (4%)
    pallas_call x1, Pallas kernels, local(): pl.pallas_call(functools.partial(kernel, sizes), out_shape=(jax.ShapeDtyp...  107 us
    unnamed x4, local copies, waits for them, and re-layouts  4.55 us

commit v1 on v0

v1 whole, which is shorter than its diff:
```python
import functools
import jax
import jax.numpy as jnp
from jax import lax
from jax.experimental import pallas as pl
from jax.experimental.pallas import tpu as pltpu
from jax.sharding import PartitionSpec as P

B = 128
SW = 512
CHUNKS = 8
OCHUNKS = 4
TM = 256
F32 = jnp.float32
BF = jnp.bfloat16
MESH = pl.DeviceIdType.MESH
NN = (((1,), (0,)), ((), ()))
NT = (((1,), (1,)), ((), ()))


def split(value):
    high = value.astype(BF)
    return high, (value - high.astype(F32)).astype(BF)


def dot3(ah, al, bh, bl, dims):
    dot = functools.partial(lax.dot_general, dimension_numbers=dims, preferred_element_type=F32)
    return dot(ah, bh) + (dot(ah, bl) + dot(al, bh))


def packed_rows(nrow):
    wb = SW // B
    return (wb * (wb + 1) // 2 - wb // 2) * B + 8 * nrow


def factor(count):
    low = 1
    for value in range(1, count + 1):
        if count % value == 0 and value * value <= count:
            low = value
    return count // low, low


class Group:
    def __init__(self, copies):
        self.copies = copies

    def start(self):
        for one in self.copies:
            one.start()

    def wait_recv(self):
        for one in self.copies:
            one.wait_recv()

    def wait_send(self):
        for one in self.copies:
            one.wait_send()


def kernel(
    sizes,
    anc_ref, panel_ref, diag_ref, widths_ref, pattern_ref, prod_ref, upd_ref,
    anc, ah, al, ph, plo, pin, opp, oh, ol, qsend, qrecv, upack, urecv, usum, urecv2, ufin,
    zs, zr, ps, pr, os_, or_, qs, qr, us, ur, us2, ur2, gs2, gr2, gs, gr, ds, crossed,
):
    nsec, nrow, ncol, nf, ns, nb, square = sizes
    rows, width = panel_ref.shape
    pw = anc_ref.shape[1]
    per = width // pw
    slots = rows // SW
    wb = SW // B
    part = packed_rows(nrow) // nrow
    tm = TM
    parts = SW // tm
    sec, row, col = lax.axis_index("sec"), lax.axis_index("row"), lax.axis_index("col")
    turn = sec if square else 0
    a, b = row // nb, row % nb
    f = a + turn * (b - a)
    s = b + turn * (a - b)
    cf = nb - turn * (nb - 1)
    cs = 1 + turn * (nb - 1)

    def at(fi, si):
        return fi * cf + si * cs

    def copy(src, dst, send, recv, where):
        return pltpu.make_async_remote_copy(
            src_ref=src, dst_ref=dst, send_sem=send, recv_sem=recv, device_id=where, device_id_type=MESH
        )

    first = (sec * ncol + col) * slots
    blocks = width // B
    fill = [widths_ref[first + j] for j in range(slots)]
    load_diag = pltpu.make_async_copy(diag_ref, upd_ref, ds)

    def inside(j, i):
        return jnp.where(fill[j] > i, 1.0, 0.0).astype(F32)

    def present(j, r, c):
        return pattern_ref[first + j, r * blocks + c].astype(F32)

    def keep(src, j, h, slot, r):
        for i in range(h * wb // parts, (h + 1) * wb // parts):
            here = pl.ds(j * SW + i * B, B)
            for c in range(blocks):
                cols = pl.ds(c * B, B)
                high, low = split(src(i, cols) * (inside(j, i) * present(j, r, c)))
                ph[slot, here, cols] = high
                plo[slot, here, cols] = low

    has_left = (col > 0).astype(jnp.int32)
    has_right = (col < ncol - 1).astype(jnp.int32)
    barrier = pltpu.get_barrier_semaphore()
    for d in range(1, nrow):
        pl.semaphore_signal(barrier, inc=1, device_id={"row": (row + d) % nrow}, device_id_type=MESH)
    pl.semaphore_signal(barrier, inc=1, device_id={"sec": 1 - sec}, device_id_type=MESH)

    @pl.when(col > 0)
    def _():
        pl.semaphore_signal(barrier, inc=1, device_id={"col": col - 1}, device_id_type=MESH)

    @pl.when(col < ncol - 1)
    def _():
        pl.semaphore_signal(barrier, inc=1, device_id={"col": col + 1}, device_id_type=MESH)

    pl.semaphore_wait(barrier, nrow + has_left + has_right)

    mine = sec * ncol + col

    def piece_copy(src, p, way):
        where = ({"col": col - 1}, {"col": col + 1}, {"sec": 1 - sec})[way]
        size = src.shape[0] // CHUNKS
        return Group([
            copy(
                src.at[pl.ds(c * size, size)], anc.at[p, pl.ds(c * size, size)],
                zs.at[p, way, c], zr.at[p, c], where,
            )
            for c in range(CHUNKS)
        ])

    def opp_copy(src, d, e, k):
        return copy(
            src, opp.at[d - 1, e - 1, k], os_.at[d - 1, e - 1, k], or_.at[d - 1, e - 1, k],
            {"row": at((f + d) % nf, s)},
        )

    def pass_on(src, p):
        for d in range(1, nf):
            for e in range(1, ns):
                @pl.when(p // per == at((f + d) % nf, (s + e) % ns))
                def _():
                    opp_copy(src, d, e, p % per).start()

    def panel_copy(d, j, h):
        return copy(
            panel_ref.at[pl.ds(j * SW + h * tm, tm)], pin.at[d - 1, j, pl.ds(h * tm, tm)],
            ps.at[d - 1, j, h], pr.at[d - 1, j, h], {"row": at((f + d) % nf, s)},
        )

    def halves(src, p):
        high, low = split(src[...])
        ah[p] = high
        al[p] = low

    def late(p):
        return p // per == row

    def send_mine():
        pl.when(col > 0)(lambda: piece_copy(anc_ref, mine, 0).start())
        pl.when(col < ncol - 1)(lambda: piece_copy(anc_ref, mine, 1).start())
        piece_copy(anc_ref, mine, 2).start()

    other = (1 - sec) * ncol + col

    def panels_out():
        for j in range(slots):
            for h in range(parts):
                for d in range(1, nf):
                    panel_copy(d, j, h).start()

    def settle_own():
        load_diag.start()
        halves(anc_ref, mine)
        for j in range(slots):
            for h in range(parts):
                keep(lambda i, cols: panel_ref[pl.ds(j * SW + i * B, B), cols], j, h, 0, row)

    def relay(p, way, c, onward):
        piece_copy(anc_ref, p, way).copies[c].wait_recv()
        pl.when(onward)(lambda: piece_copy(anc.at[p], p, way).copies[c].start())
        piece_copy(anc.at[p], p, 2).copies[c].start()

    if crossed is not None:
        obuf, xs, xr, zos, zor = crossed
        half = width // 2
        osize = half // OCHUNKS

        def native(z):
            return (z // per != b).astype(jnp.int32)

        def early(side, z):
            return native(z) == (side == a).astype(jnp.int32)

        def cross_copies(axis):
            where = {"row": (1 - a) * nb + b} if axis == 0 else {"row": a * nb + 1 - b}
            k = col % per
            base = (k if axis == 0 else 1 - k) * half
            return Group([
                copy(
                    anc_ref.at[pl.ds(pl.multiple_of(base + c * osize, 8), osize)],
                    obuf.at[col, pl.ds(c * osize, osize)], xs.at[axis, c], xr.at[c], where,
                )
                for c in range(OCHUNKS)
            ])

        def o_copy(z, way):
            where = ({"col": col - 1}, {"col": col + 1}, {"sec": 1 - sec})[way]
            return Group([
                copy(
                    obuf.at[z, pl.ds(c * osize, osize)], obuf.at[z, pl.ds(c * osize, osize)],
                    zos.at[z, way, c], zor.at[z, c], where,
                )
                for c in range(OCHUNKS)
            ])

        is_early = early(sec, col)
        is_opp = jnp.logical_and(native(col) == 1, sec != a)

        @pl.when(is_opp)
        def _():
            cross_copies(0).start()
            cross_copies(1).start()

        pl.when(is_early)(send_mine)
        panels_out()
        settle_own()

        @pl.when(is_early)
        def _():
            for c in range(OCHUNKS):
                cross_copies(0).copies[c].wait_recv()
                pl.when(col > 0)(lambda: o_copy(col, 0).copies[c].start())
                pl.when(col < ncol - 1)(lambda: o_copy(col, 1).copies[c].start())
                o_copy(col, 2).copies[c].start()

        def o_relay(z, way, c, onward):
            o_copy(z, way).copies[c].wait_recv()
            pl.when(onward)(lambda: o_copy(z, way).copies[c].start())
            o_copy(z, 2).copies[c].start()

        def from_partner(z):
            p = (1 - sec) * ncol + z
            piece_copy(anc_ref, p, 2).wait_recv()
            o_copy(z, 2).wait_recv()
            halves(anc.at[p], p)

        def early_step(t, carry):
            left = jnp.logical_and(col - t >= 0, early(sec, col - t))
            right = jnp.logical_and(col + t < ncol, early(sec, col + t))
            for c in range(CHUNKS):
                pl.when(left)(lambda: relay(mine - t, 1, c, col < ncol - 1))
                pl.when(right)(lambda: relay(mine + t, 0, c, col > 0))
            for c in range(OCHUNKS):
                pl.when(left)(lambda: o_relay(col - t, 1, c, col < ncol - 1))
                pl.when(right)(lambda: o_relay(col + t, 0, c, col > 0))
            pl.when(left)(lambda: halves(anc.at[mine - t], mine - t))
            pl.when(right)(lambda: halves(anc.at[mine + t], mine + t))
            left = jnp.logical_and(col - t >= 0, early(1 - sec, col - t))
            right = jnp.logical_and(col + t < ncol, early(1 - sec, col + t))
            pl.when(left)(lambda: from_partner(col - t))
            pl.when(right)(lambda: from_partner(col + t))
            return carry

        pl.when(early(1 - sec, col))(lambda: from_partner(col))
        lax.fori_loop(1, ncol, early_step, 0)
        pl.when(late(mine))(send_mine)

        for z in range(ncol):
            k = z % per
            seen = native(z)
            turned = seen == sec
            rpos = jnp.where(jnp.logical_or(seen == 1, sec == 0), k, 1 - k)
            cpos = jnp.where(jnp.logical_or(seen == 1, sec == 1), k, 1 - k)
            here = pl.ds(pl.multiple_of(rpos * half, half), half)

            def place(value):
                high, low = split(value)
                oh[0, 0, cpos, here] = high
                ol[0, 0, cpos, here] = low

            pl.when(turned)(lambda: place(obuf[z].T))
            pl.when(jnp.logical_not(turned))(lambda: place(obuf[z]))

        def late_partner(p):
            piece_copy(anc_ref, p, 2).wait_recv()
            halves(anc.at[p], p)

        def late_step(t):
            left = jnp.logical_and(col - t >= 0, late(mine - t))
            right = jnp.logical_and(col + t < ncol, late(mine + t))
            for c in range(CHUNKS):
                pl.when(left)(lambda: relay(mine - t, 1, c, col < ncol - 1))
                pl.when(right)(lambda: relay(mine + t, 0, c, col > 0))
            pl.when(left)(lambda: halves(anc.at[mine - t], mine - t))
            pl.when(right)(lambda: halves(anc.at[mine + t], mine + t))
            left = jnp.logical_and(col - t >= 0, late(other - t))
            right = jnp.logical_and(col + t < ncol, late(other + t))
            pl.when(left)(lambda: late_partner(other - t))
            pl.when(right)(lambda: late_partner(other + t))

        def late_work(spot):
            if spot == 0:
                pl.when(late(other))(lambda: late_partner(other))
            elif spot < slots * parts:
                if spot < ncol:
                    late_step(spot)

        def late_rest():
            for t in range(slots * parts, ncol):
                late_step(t)
    else:
        @pl.when(jnp.logical_not(late(mine)))
        def _():
            send_mine()
            pass_on(anc_ref, mine)

        panels_out()
        settle_own()

        def settle(p):
            pass_on(anc.at[p], p)
            halves(anc.at[p], p)

        def from_partner(p):
            piece_copy(anc_ref, p, 2).wait_recv()
            pass_on(anc.at[p], p)
            halves(anc.at[p], p)

        def gather(phase):
            def ready(p):
                return late(p) if phase else jnp.logical_not(late(p))

            def step(t, carry):
                left = jnp.logical_and(col - t >= 0, ready(mine - t))
                right = jnp.logical_and(col + t < ncol, ready(mine + t))
                for c in range(CHUNKS):
                    pl.when(left)(lambda: relay(mine - t, 1, c, col < ncol - 1))
                    pl.when(right)(lambda: relay(mine + t, 0, c, col > 0))
                pl.when(left)(lambda: settle(mine - t))
                pl.when(right)(lambda: settle(mine + t))
                partners(t)
                return carry

            def partners(t):
                left = jnp.logical_and(col - t >= 0, ready(other - t))
                right = jnp.logical_and(col + t < ncol, ready(other + t))
                pl.when(left)(lambda: from_partner(other - t))
                pl.when(jnp.logical_and(right, t > 0))(lambda: from_partner(other + t))

            partners(0)
            lax.fori_loop(1, ncol, step, 0)

        gather(0)
        pl.when(late(mine))(send_mine)
        for d in range(1, nf):
            for e in range(1, ns):
                for k in range(per):
                    opp_copy(anc_ref, d, e, k).wait_recv()
                    high, low = split(opp[d - 1, e - 1, k])
                    oh[d - 1, e - 1, k] = high
                    ol[d - 1, e - 1, k] = low

        def late_work(spot):
            pass

        def late_rest():
            gather(1)

    def q_copy(e, j, h):
        rr = pl.ds(h * tm, tm)
        return copy(
            qsend.at[e - 1, j, rr], qrecv.at[e - 1, j, rr], qs.at[e - 1, j, h], qr.at[e - 1, j, h],
            {"row": at(f, (s + e) % ns)},
        )

    for j in range(slots):
        for h in range(parts):
            for d in range(1, nf):
                panel_copy(d, j, h).wait_recv()
                keep(lambda i, cols: pin[d - 1, j, pl.ds(i * B, B), cols], j, h, d, at((f + nf - d) % nf, s))
            rr = pl.ds(j * SW + h * tm, tm)
            for e in range(1, ns):
                base = at(f, (s + e) % ns) * per
                for k in range(per):
                    acc = dot3(ph[0, rr], plo[0, rr], ah[base + k], al[base + k], NN)
                    for d in range(1, nf):
                        acc += dot3(ph[d, rr], plo[d, rr], oh[d - 1, e - 1, k], ol[d - 1, e - 1, k], NN)
                    qsend[e - 1, j, pl.ds(h * tm, tm), pl.ds(k * pw, pw)] = acc
                q_copy(e, j, h).start()
            late_work(j * parts + h)

    def near(i, carry):
        rr = pl.ds(pl.multiple_of(i * tm, tm), tm)
        acc = jnp.zeros((tm, width), F32)
        for d in range(1, nf):
            for k in range(per):
                p = at((f + nf - d) % nf, s) * per + k
                cols = pl.ds(k * pw, pw)
                acc += dot3(ph[d, rr, cols], plo[d, rr, cols], ah[p], al[p], NT)
        prod_ref[rr] = acc
        return carry

    lax.fori_loop(0, rows // tm, near, 0)
    late_rest()

    def own(i, carry):
        rr = pl.ds(pl.multiple_of(i * tm, tm), tm)
        for k in range(per):
            p = row * per + k
            prod_ref[rr, pl.ds(k * pw, pw)] += dot3(ph[0, rr], plo[0, rr], ah[p], al[p], NN)
        return carry

    lax.fori_loop(0, rows // tm, own, 0)

    span = nf * part

    def portion(i):
        return pl.ds(pl.multiple_of(i * span, 8), span)

    def across(d):
        return {"row": at(f, (s + d) % ns)}

    def along(d):
        return {"row": at((f + d) % nf, s)}

    def u_copy(j, d):
        return copy(
            upack.at[j, portion((s + d) % ns)], urecv.at[j, d - 1], us.at[j, d - 1], ur.at[j, d - 1], across(d)
        )

    def v_copy(j, d):
        return copy(
            usum.at[j, pl.ds(pl.multiple_of(((f + d) % nf) * part, 8), part)],
            urecv2.at[j, d - 1], us2.at[j, d - 1], ur2.at[j, d - 1], along(d),
        )

    def h_copy(j, d):
        done = pl.ds(pl.multiple_of((s * nf + f) * part, 8), part)
        return copy(ufin.at[j, done], ufin.at[j, done], gs2.at[j, d - 1], gr2.at[j, d - 1], along(d))

    def g_copy(j, d):
        return copy(ufin.at[j, portion(s)], ufin.at[j, portion(s)], gs.at[j, d - 1], gr.at[j, d - 1], across(d))

    ri = lax.broadcasted_iota(jnp.int32, (B, B), 0)
    ci = lax.broadcasted_iota(jnp.int32, (B, B), 1)
    rows8 = lax.broadcasted_iota(jnp.int32, (8, B), 0)
    pairs = wb // 2
    offs = {}
    for i in range(wb):
        for k in range(i + 1, wb):
            offs[i, k] = (pairs + len(offs)) * B
    tail = (pairs + len(offs)) * B

    def update_out(j):
        for h in range(parts):
            rr = pl.ds(j * SW + h * tm, tm)
            for e in range(1, ns):
                q_copy(e, j, h).wait_recv()
                prod_ref[rr] += qrecv[e - 1, j, pl.ds(h * tm, tm)]
        extra = jnp.zeros((8, B), F32)
        held = None
        for i in range(wb):
            qh, ql = split(prod_ref[pl.ds(j * SW + i * B, B)])
            rest = pl.ds(j * SW + i * B, SW - i * B)
            line = dot3(qh, ql, ph[0, rest], plo[0, rest], NT)
            for k in range(i + 1, wb):
                upack[j, pl.ds(offs[i, k], B)] = line[:, (k - i) * B:(k - i + 1) * B]
            if i % 2 == 0:
                held = line[:, :B]
            else:
                low = line[:, :B]
                upack[j, pl.ds(i // 2 * B, B)] = jnp.where(ri <= ci, held, low)
                mid = jnp.sum(jnp.where(ri == ci, low, 0.0), axis=0, keepdims=True)
                extra = jnp.where(rows8 == i // 2, mid, extra)
        upack[j, pl.ds(tail, 8)] = extra
        upack[j, pl.ds(tail + 8, 8 * (nrow - 1))] = jnp.zeros((8 * (nrow - 1), B), F32)
        for d in range(1, ns):
            u_copy(j, d).start()

    def second(j):
        for d in range(1, ns):
            u_copy(j, d).wait_recv()
        total = upack[j, portion(s)]
        for d in range(1, ns):
            total += urecv[j, d - 1]
        usum[j] = total
        for d in range(1, nf):
            v_copy(j, d).start()

    def third(j):
        for d in range(1, nf):
            v_copy(j, d).wait_recv()
        total = usum[j, pl.ds(pl.multiple_of(f * part, 8), part)]
        for d in range(1, nf):
            total += urecv2[j, d - 1]
        ufin[j, pl.ds(pl.multiple_of((s * nf + f) * part, 8), part)] = total
        for d in range(1, nf):
            h_copy(j, d).start()

    def fourth(j):
        for d in range(1, nf):
            h_copy(j, d).wait_recv()
        for d in range(1, ns):
            g_copy(j, d).start()

    def negate(j):
        for i in range(wb):
            here = pl.ds(j * SW + i * B, B)
            for c in range(blocks):
                cols = pl.ds(c * B, B)
                prod_ref[here, cols] = prod_ref[here, cols] * -(inside(j, i) * present(j, row, c))

    def finish(j):
        for d in range(1, ns):
            g_copy(j, d).wait_recv()
        for i in range(wb):
            both = ufin[j, pl.ds(i // 2 * B, B)]
            if i % 2 == 0:
                block = jnp.where(ri <= ci, both, both.T)
            else:
                block = jnp.where(ri > ci, both, both.T)
                block = jnp.where(ri == ci, ufin[j, pl.ds(tail + i // 2, 1)], block)
            here = (pl.ds(j * SW + i * B, B), pl.ds(i * B, B))
            upd_ref[here] = (upd_ref[here] + block) * inside(j, i)
            for k in range(i + 1, wb):
                block = ufin[j, pl.ds(offs[i, k], B)]
                upper = (pl.ds(j * SW + i * B, B), pl.ds(k * B, B))
                upd_ref[upper] = (upd_ref[upper] + block) * inside(j, k)
                lower = (pl.ds(j * SW + k * B, B), pl.ds(i * B, B))
                upd_ref[lower] = (upd_ref[lower] + block.T) * inside(j, k)

    stages = [update_out, second, third, fourth]
    for step in range(2 * (slots - 1) + len(stages)):
        for j in range(slots):
            if 0 <= step - 2 * j < len(stages):
                stages[step - 2 * j](j)
    for j in range(slots):
        negate(j)
    load_diag.wait()
    for j in range(slots):
        finish(j)

    for j in range(slots):
        for d in range(1, ns):
            u_copy(j, d).wait_send()
            g_copy(j, d).wait_send()
        for d in range(1, nf):
            v_copy(j, d).wait_send()
            h_copy(j, d).wait_send()
        for h in range(parts):
            for e in range(1, ns):
                q_copy(e, j, h).wait_send()
            for d in range(1, nf):
                panel_copy(d, j, h).wait_send()

    if crossed is None:
        for d in range(1, nf):
            for e in range(1, ns):
                for k in range(per):
                    opp_copy(anc_ref, d, e, k).wait_send()

    def drain(q, carry):
        p = sec * ncol + q
        to_right = jnp.logical_and(q <= col, col < ncol - 1)
        to_left = jnp.logical_and(q >= col, col > 0)
        if crossed is None:
            sent = q >= 0
        else:
            sent = jnp.logical_or(early(sec, q), late(p))
        pl.when(jnp.logical_and(sent, to_right))(lambda: piece_copy(anc_ref, p, 1).wait_send())
        pl.when(jnp.logical_and(sent, to_left))(lambda: piece_copy(anc_ref, p, 0).wait_send())
        pl.when(sent)(lambda: piece_copy(anc_ref, p, 2).wait_send())
        if crossed is not None:
            first_half = early(sec, q)
            pl.when(jnp.logical_and(first_half, to_right))(lambda: o_copy(q, 1).wait_send())
            pl.when(jnp.logical_and(first_half, to_left))(lambda: o_copy(q, 0).wait_send())
            pl.when(first_half)(lambda: o_copy(q, 2).wait_send())
        return carry

    lax.fori_loop(0, ncol, drain, 0)
    if crossed is not None:
        @pl.when(is_opp)
        def _():
            cross_copies(0).wait_send()
            cross_copies(1).wait_send()


def local(sizes, anc_inverse, panel, diag_inverse, widths, pattern):
    nsec, nrow, ncol, nf, ns, nb, square = sizes
    rows, width = panel.shape
    pw = anc_inverse.shape[1]
    per = width // pw
    slots = rows // SW
    pieces = nsec * ncol
    packed = packed_rows(nrow)
    part = packed // nrow
    parts = SW // TM
    short = square and nsec == nb == per == 2 and ncol == per * nb
    vm = pltpu.VMEM
    dma = pltpu.SemaphoreType.DMA
    whole = pl.BlockSpec(memory_space=pltpu.VMEM)
    scalar = pl.BlockSpec(memory_space=pltpu.SMEM)
    return pl.pallas_call(
        functools.partial(kernel, sizes),
        out_shape=(jax.ShapeDtypeStruct((rows, width), F32), jax.ShapeDtypeStruct((rows, SW), F32)),
        in_specs=[whole, whole, pl.BlockSpec(memory_space=pl.ANY), scalar, scalar],
        out_specs=(whole, whole),
        scratch_shapes=[
            vm((pieces, width, pw), F32),
            vm((pieces, width, pw), BF),
            vm((pieces, width, pw), BF),
            vm((nf, rows, width), BF),
            vm((nf, rows, width), BF),
            vm((nf - 1, slots, SW, width), F32),
            None if short else vm((nf - 1, ns - 1, per, width, pw), F32),
            vm((nf - 1, ns - 1, per, width, pw), BF),
            vm((nf - 1, ns - 1, per, width, pw), BF),
            vm((ns - 1, slots, SW, width), F32),
            vm((ns - 1, slots, SW, width), F32),
            vm((slots, packed, B), F32),
            vm((slots, ns - 1, nf * part, B), F32),
            vm((slots, nf * part, B), F32),
            vm((slots, nf - 1, part, B), F32),
            vm((slots, packed, B), F32),
            dma((pieces, 3, CHUNKS)), dma((pieces, CHUNKS)),
            dma((nf - 1, slots, parts)), dma((nf - 1, slots, parts)),
            None if short else dma((nf - 1, ns - 1, per)), None if short else dma((nf - 1, ns - 1, per)),
            dma((ns - 1, slots, parts)), dma((ns - 1, slots, parts)),
            dma((slots, ns - 1)), dma((slots, ns - 1)),
            dma((slots, nf - 1)), dma((slots, nf - 1)),
            dma((slots, nf - 1)), dma((slots, nf - 1)),
            dma((slots, ns - 1)), dma((slots, ns - 1)),
            dma,
            (
                vm((ncol, width // 2, pw), F32), dma((2, OCHUNKS)), dma((OCHUNKS,)),
                dma((ncol, 3, OCHUNKS)), dma((ncol, OCHUNKS)),
            ) if short else None,
        ],
        compiler_params=pltpu.CompilerParams(
            collective_id=0, has_side_effects=True, vmem_limit_bytes=60 * 1024 * 1024
        ),
    )(anc_inverse, panel, diag_inverse, widths, pattern)


def solution(mesh):
    shape = dict(mesh.shape)
    na, nb = factor(shape["row"])
    sizes = (shape["sec"], shape["row"], shape["col"], na, nb, nb, na == nb)
    in_specs = (
        P("row", ("sec", "col")),
        P(("sec", "col"), "row"),
        P(("sec", "col"), None),
        P(),
        P(),
    )
    out_specs = (P(("sec", "col"), "row"), P(("sec", "col"), None))
    return jax.shard_map(
        functools.partial(local, sizes), mesh=mesh, in_specs=in_specs, out_specs=out_specs, check_vma=False
    )
```

time: 114 us -> 102 us (0.89)
  the two profiles are of different devices: /device:TPU:0 before, /device:TPU:30 now
where the time goes in v1:
time: 102 us
  Pallas kernels  97 us (95%)
  local copies, waits for them, and re-layouts  4.55 us (4%)
    pallas_call x1, Pallas kernels, local(): pl.pallas_call(functools.partial(kernel, sizes), out_shape=(jax.ShapeDtyp...  97 us
    unnamed x4, local copies, waits for them, and re-layouts  4.55 us

profile of v1, /device:TPU:30, one launch (start us, length us, event | category | flops | bytes accessed | tf_op | source)
XLA Modules:
  0.0 102.2 jit_solution(8424233002546805757)
XLA Ops:
  0.6 97.0 %shard_map.68 = (f32[1024,512]{1,0:T(8,128)}, f32[1024,512]{1,0:T(8,128)}) custom-call(f32[512,256]{1,0:T(8,128)} %anc_ref.1, f32[1024,512]{1,0:T(8,128)} %panel_ref.1, f32[1024,512]{1,0:T(8,128)} %diag_ref.1, s32[16]{0:T(128)} %widths_ref.1, s32[16,16]{1,0:T(8,128)} %pattern_ref.1), custom_call_target="tpu_custom_call" | custom-call | tf_op jit(solution)/shard_map/pallas_call | solution.py:614
  97.6 0.0 copy-start
  97.6 3.2 %copy.9 = f32[1024,512]{1,0:T(8,128)} copy(f32[1024,512]{1,0:T(8,128)} %get-tuple-element.4) | data formatting | bytes 4194304
  100.9 0.0 copy-done
  100.9 1.3 %copy.10 = f32[1024,512]{1,0:T(8,128)} copy(f32[1024,512]{1,0:T(8,128)S(1)} %copy-done) | data formatting | bytes 4194304
Async XLA Ops:
  97.6 3.2 %copy-start = (f32[1024,512]{1,0:T(8,128)S(1)}, f32[1024,512]{1,0:T(8,128)}, u32[]{:S(2)}) copy-start(f32[1024,512]{1,0:T(8,128)} %get-tuple-element.5) | copy-start | bytes 6291460

commit v2 on v1

--- a/solution.py
+++ b/solution.py
@@ -33,6 +33,14 @@
     return (wb * (wb + 1) // 2 - wb // 2) * B + 8 * nrow
 
 
+def spots(wb):
+    offs = {}
+    for i in range(wb):
+        for k in range(i + 1, wb):
+            offs[i, k] = (wb // 2 + len(offs)) * B
+    return offs, (wb // 2 + len(offs)) * B
+
+
 def factor(count):
     low = 1
     for value in range(1, count + 1):
@@ -60,9 +68,9 @@
 
 def kernel(
     sizes,
-    anc_ref, panel_ref, diag_ref, widths_ref, pattern_ref, prod_ref, upd_ref,
+    anc_ref, panel_ref, widths_ref, pattern_ref, prod_ref, sum_ref,
     anc, ah, al, ph, plo, pin, opp, oh, ol, qsend, qrecv, upack, urecv, usum, urecv2, ufin,
-    zs, zr, ps, pr, os_, or_, qs, qr, us, ur, us2, ur2, gs2, gr2, gs, gr, ds, crossed,
+    zs, zr, ps, pr, os_, or_, qs, qr, us, ur, us2, ur2, gs2, gr2, gs, gr, crossed,
 ):
     nsec, nrow, ncol, nf, ns, nb, square = sizes
     rows, width = panel_ref.shape
@@ -92,7 +100,6 @@
     first = (sec * ncol + col) * slots
     blocks = width // B
     fill = [widths_ref[first + j] for j in range(slots)]
-    load_diag = pltpu.make_async_copy(diag_ref, upd_ref, ds)
 
     def inside(j, i):
         return jnp.where(fill[j] > i, 1.0, 0.0).astype(F32)
@@ -180,7 +187,6 @@
                     panel_copy(d, j, h).start()
 
     def settle_own():
-        load_diag.start()
         halves(anc_ref, mine)
         for j in range(slots):
             for h in range(parts):
@@ -232,8 +238,10 @@
             cross_copies(0).start()
             cross_copies(1).start()
 
+        at_end = jnp.logical_or(col == 0, col == ncol - 1)
         pl.when(is_early)(send_mine)
         panels_out()
+        pl.when(jnp.logical_and(late(mine), at_end))(send_mine)
         settle_own()
 
         @pl.when(is_early)
@@ -272,53 +280,48 @@
             pl.when(right)(lambda: from_partner(col + t))
             return carry
 
-        pl.when(early(1 - sec, col))(lambda: from_partner(col))
-        lax.fori_loop(1, ncol, early_step, 0)
-        pl.when(late(mine))(send_mine)
-
-        for z in range(ncol):
+        def spot(z):
+            k = z % per
+            return jnp.where(jnp.logical_or(native(z) == 1, sec == 1), k, 1 - k)
+
+        def place(z):
             k = z % per
             seen = native(z)
             turned = seen == sec
             rpos = jnp.where(jnp.logical_or(seen == 1, sec == 0), k, 1 - k)
-            cpos = jnp.where(jnp.logical_or(seen == 1, sec == 1), k, 1 - k)
             here = pl.ds(pl.multiple_of(rpos * half, half), half)
 
-            def place(value):
+            def put(value):
                 high, low = split(value)
-                oh[0, 0, cpos, here] = high
-                ol[0, 0, cpos, here] = low
-
-            pl.when(turned)(lambda: place(obuf[z].T))
-            pl.when(jnp.logical_not(turned))(lambda: place(obuf[z]))
+                oh[0, 0, spot(z), here] = high
+                ol[0, 0, spot(z), here] = low
+
+            pl.when(turned)(lambda: put(obuf[z].T))
+            pl.when(jnp.logical_not(turned))(lambda: put(obuf[z]))
 
         def late_partner(p):
             piece_copy(anc_ref, p, 2).wait_recv()
             halves(anc.at[p], p)
 
-        def late_step(t):
-            left = jnp.logical_and(col - t >= 0, late(mine - t))
-            right = jnp.logical_and(col + t < ncol, late(mine + t))
+        def late_step(t, ends):
+            def wanted(p, z):
+                edge = jnp.logical_or(z == 0, z == ncol - 1)
+                return jnp.logical_and(late(p), edge if ends else jnp.logical_not(edge))
+
+            left = jnp.logical_and(col - t >= 0, wanted(mine - t, col - t))
+            right = jnp.logical_and(col + t < ncol, wanted(mine + t, col + t))
             for c in range(CHUNKS):
                 pl.when(left)(lambda: relay(mine - t, 1, c, col < ncol - 1))
                 pl.when(right)(lambda: relay(mine + t, 0, c, col > 0))
             pl.when(left)(lambda: halves(anc.at[mine - t], mine - t))
             pl.when(right)(lambda: halves(anc.at[mine + t], mine + t))
+
+        def late_partners(t):
             left = jnp.logical_and(col - t >= 0, late(other - t))
             right = jnp.logical_and(col + t < ncol, late(other + t))
             pl.when(left)(lambda: late_partner(other - t))
             pl.when(right)(lambda: late_partner(other + t))
 
-        def late_work(spot):
-            if spot == 0:
-                pl.when(late(other))(lambda: late_partner(other))
-            elif spot < slots * parts:
-                if spot < ncol:
-                    late_step(spot)
-
-        def late_rest():
-            for t in range(slots * parts, ncol):
-                late_step(t)
     else:
         @pl.when(jnp.logical_not(late(mine)))
         def _():
@@ -371,34 +374,45 @@
                     oh[d - 1, e - 1, k] = high
                     ol[d - 1, e - 1, k] = low
 
-        def late_work(spot):
-            pass
-
-        def late_rest():
-            gather(1)
-
-    def q_copy(e, j, h):
-        rr = pl.ds(h * tm, tm)
+    def q_copy(e, k, j, h):
+        rr = pl.ds(j * SW + h * tm, tm)
         return copy(
-            qsend.at[e - 1, j, rr], qrecv.at[e - 1, j, rr], qs.at[e - 1, j, h], qr.at[e - 1, j, h],
+            qsend.at[e - 1, k, rr], qrecv.at[e - 1, k, rr], qs.at[e - 1, k, j, h], qr.at[e - 1, k, j, h],
             {"row": at(f, (s + e) % ns)},
         )
 
-    for j in range(slots):
-        for h in range(parts):
-            for d in range(1, nf):
-                panel_copy(d, j, h).wait_recv()
-                keep(lambda i, cols: pin[d - 1, j, pl.ds(i * B, B), cols], j, h, d, at((f + nf - d) % nf, s))
-            rr = pl.ds(j * SW + h * tm, tm)
-            for e in range(1, ns):
-                base = at(f, (s + e) % ns) * per
-                for k in range(per):
-                    acc = dot3(ph[0, rr], plo[0, rr], ah[base + k], al[base + k], NN)
+    def products(k, fresh):
+        for j in range(slots):
+            for h in range(parts):
+                rr = pl.ds(j * SW + h * tm, tm)
+                for d in range(1, nf):
+                    if fresh:
+                        panel_copy(d, j, h).wait_recv()
+                        keep(lambda i, cols: pin[d - 1, j, pl.ds(i * B, B), cols], j, h, d, at((f + nf - d) % nf, s))
+                for e in range(1, ns):
+                    p = at(f, (s + e) % ns) * per + k
+                    acc = dot3(ph[0, rr], plo[0, rr], ah[p], al[p], NN)
                     for d in range(1, nf):
                         acc += dot3(ph[d, rr], plo[d, rr], oh[d - 1, e - 1, k], ol[d - 1, e - 1, k], NN)
-                    qsend[e - 1, j, pl.ds(h * tm, tm), pl.ds(k * pw, pw)] = acc
-                q_copy(e, j, h).start()
-            late_work(j * parts + h)
+                    qsend[e - 1, k, rr] = acc
+                    q_copy(e, k, j, h).start()
+
+    if crossed is not None:
+        last = ncol - 1 - col
+        pl.when(early(1 - sec, col))(lambda: from_partner(col))
+        lax.fori_loop(1, ncol - 1, early_step, 0)
+        pl.when(jnp.logical_and(late(mine), jnp.logical_not(at_end)))(send_mine)
+        late_step(1, True)
+        for z in range(ncol):
+            pl.when(z != last)(functools.partial(place, z))
+        products(1 - spot(last), True)
+        early_step(ncol - 1, 0)
+        place(last)
+        products(spot(last), False)
+        late_step(1, False)
+    else:
+        for k in range(per):
+            products(k, k == 0)
 
     def near(i, carry):
         rr = pl.ds(pl.multiple_of(i * tm, tm), tm)
@@ -412,7 +426,15 @@
         return carry
 
     lax.fori_loop(0, rows // tm, near, 0)
-    late_rest()
+    if crossed is not None:
+        pl.when(late(other))(lambda: late_partner(other))
+        late_partners(1)
+        for t in range(2, ncol):
+            late_step(t, True)
+            late_step(t, False)
+            late_partners(t)
+    else:
+        gather(1)
 
     def own(i, carry):
         rr = pl.ds(pl.multiple_of(i * tm, tm), tm)
@@ -455,19 +477,15 @@
     ri = lax.broadcasted_iota(jnp.int32, (B, B), 0)
     ci = lax.broadcasted_iota(jnp.int32, (B, B), 1)
     rows8 = lax.broadcasted_iota(jnp.int32, (8, B), 0)
-    pairs = wb // 2
-    offs = {}
-    for i in range(wb):
-        for k in range(i + 1, wb):
-            offs[i, k] = (pairs + len(offs)) * B
-    tail = (pairs + len(offs)) * B
+    offs, tail = spots(wb)
 
     def update_out(j):
         for h in range(parts):
             rr = pl.ds(j * SW + h * tm, tm)
             for e in range(1, ns):
-                q_copy(e, j, h).wait_recv()
-                prod_ref[rr] += qrecv[e - 1, j, pl.ds(h * tm, tm)]
+                for k in range(per):
+                    q_copy(e, k, j, h).wait_recv()
+                    prod_ref[rr, pl.ds(k * pw, pw)] += qrecv[e - 1, k, rr]
         extra = jnp.zeros((8, B), F32)
         held = None
         for i in range(wb):
@@ -514,31 +532,10 @@
         for d in range(1, ns):
             g_copy(j, d).start()
 
-    def negate(j):
-        for i in range(wb):
-            here = pl.ds(j * SW + i * B, B)
-            for c in range(blocks):
-                cols = pl.ds(c * B, B)
-                prod_ref[here, cols] = prod_ref[here, cols] * -(inside(j, i) * present(j, row, c))
-
     def finish(j):
         for d in range(1, ns):
             g_copy(j, d).wait_recv()
-        for i in range(wb):
-            both = ufin[j, pl.ds(i // 2 * B, B)]
-            if i % 2 == 0:
-                block = jnp.where(ri <= ci, both, both.T)
-            else:
-                block = jnp.where(ri > ci, both, both.T)
-                block = jnp.where(ri == ci, ufin[j, pl.ds(tail + i // 2, 1)], block)
-            here = (pl.ds(j * SW + i * B, B), pl.ds(i * B, B))
-            upd_ref[here] = (upd_ref[here] + block) * inside(j, i)
-            for k in range(i + 1, wb):
-                block = ufin[j, pl.ds(offs[i, k], B)]
-                upper = (pl.ds(j * SW + i * B, B), pl.ds(k * B, B))
-                upd_ref[upper] = (upd_ref[upper] + block) * inside(j, k)
-                lower = (pl.ds(j * SW + k * B, B), pl.ds(i * B, B))
-                upd_ref[lower] = (upd_ref[lower] + block.T) * inside(j, k)
+        sum_ref[j] = ufin[j]
 
     stages = [update_out, second, third, fourth]
     for step in range(2 * (slots - 1) + len(stages)):
@@ -546,9 +543,6 @@
             if 0 <= step - 2 * j < len(stages):
                 stages[step - 2 * j](j)
     for j in range(slots):
-        negate(j)
-    load_diag.wait()
-    for j in range(slots):
         finish(j)
 
     for j in range(slots):
@@ -560,7 +554,8 @@
             h_copy(j, d).wait_send()
         for h in range(parts):
             for e in range(1, ns):
-                q_copy(e, j, h).wait_send()
+                for k in range(per):
+                    q_copy(e, k, j, h).wait_send()
             for d in range(1, nf):
                 panel_copy(d, j, h).wait_send()
 
@@ -596,6 +591,47 @@
             cross_copies(1).wait_send()
 
 
+def write_out(ncol, parts, prod_ref, sum_ref, diag_ref, widths_ref, pattern_ref, off_ref, upd_ref):
+    j, h = pl.program_id(0), pl.program_id(1)
+    sec, row, col = lax.axis_index("sec"), lax.axis_index("row"), lax.axis_index("col")
+    child = (sec * ncol + col) * pl.num_programs(0) + j
+    wb = SW // B
+    each = wb // parts
+    blocks = off_ref.shape[1] // B
+    offs, tail = spots(wb)
+    ri = lax.broadcasted_iota(jnp.int32, (B, B), 0)
+    ci = lax.broadcasted_iota(jnp.int32, (B, B), 1)
+    fill = widths_ref[child]
+
+    def inside(i):
+        return jnp.where(fill > i, 1.0, 0.0).astype(F32)
+
+    for i in range(each):
+        here = pl.ds(i * B, B)
+        for c in range(blocks):
+            cols = pl.ds(c * B, B)
+            present = pattern_ref[child, row * blocks + c].astype(F32)
+            off_ref[here, cols] = prod_ref[here, cols] * -(inside(h * each + i) * present)
+
+    def block_of(i, k):
+        if i < k:
+            return sum_ref[0, pl.ds(offs[i, k], B)]
+        if i > k:
+            return sum_ref[0, pl.ds(offs[k, i], B)].T
+        both = sum_ref[0, pl.ds(i // 2 * B, B)]
+        if i % 2 == 0:
+            return jnp.where(ri <= ci, both, both.T)
+        return jnp.where(ri == ci, sum_ref[0, pl.ds(tail + i // 2, 1)], jnp.where(ri > ci, both, both.T))
+
+    for part in range(parts):
+        @pl.when(h == part)
+        def _():
+            for i in range(each):
+                for k in range(wb):
+                    here = (pl.ds(i * B, B), pl.ds(k * B, B))
+                    upd_ref[here] = (diag_ref[here] + block_of(part * each + i, k)) * inside(max(part * each + i, k))
+
+
 def local(sizes, anc_inverse, panel, diag_inverse, widths, pattern):
     nsec, nrow, ncol, nf, ns, nb, square = sizes
     rows, width = panel.shape
@@ -611,10 +647,10 @@
     dma = pltpu.SemaphoreType.DMA
     whole = pl.BlockSpec(memory_space=pltpu.VMEM)
     scalar = pl.BlockSpec(memory_space=pltpu.SMEM)
-    return pl.pallas_call(
+    product, summed = pl.pallas_call(
         functools.partial(kernel, sizes),
-        out_shape=(jax.ShapeDtypeStruct((rows, width), F32), jax.ShapeDtypeStruct((rows, SW), F32)),
-        in_specs=[whole, whole, pl.BlockSpec(memory_space=pl.ANY), scalar, scalar],
+        out_shape=(jax.ShapeDtypeStruct((rows, width), F32), jax.ShapeDtypeStruct((slots, packed, B), F32)),
+        in_specs=[whole, whole, scalar, scalar],
         out_specs=(whole, whole),
         scratch_shapes=[
             vm((pieces, width, pw), F32),
@@ -626,8 +662,8 @@
             None if short else vm((nf - 1, ns - 1, per, width, pw), F32),
             vm((nf - 1, ns - 1, per, width, pw), BF),
             vm((nf - 1, ns - 1, per, width, pw), BF),
-            vm((ns - 1, slots, SW, width), F32),
-            vm((ns - 1, slots, SW, width), F32),
+            vm((ns - 1, per, rows, pw), F32),
+            vm((ns - 1, per, rows, pw), F32),
             vm((slots, packed, B), F32),
             vm((slots, ns - 1, nf * part, B), F32),
             vm((slots, nf * part, B), F32),
@@ -636,21 +672,30 @@
             dma((pieces, 3, CHUNKS)), dma((pieces, CHUNKS)),
             dma((nf - 1, slots, parts)), dma((nf - 1, slots, parts)),
             None if short else dma((nf - 1, ns - 1, per)), None if short else dma((nf - 1, ns - 1, per)),
-            dma((ns - 1, slots, parts)), dma((ns - 1, slots, parts)),
+            dma((ns - 1, per, slots, parts)), dma((ns - 1, per, slots, parts)),
             dma((slots, ns - 1)), dma((slots, ns - 1)),
             dma((slots, nf - 1)), dma((slots, nf - 1)),
             dma((slots, nf - 1)), dma((slots, nf - 1)),
             dma((slots, ns - 1)), dma((slots, ns - 1)),
-            dma,
             (
                 vm((ncol, width // 2, pw), F32), dma((2, OCHUNKS)), dma((OCHUNKS,)),
                 dma((ncol, 3, OCHUNKS)), dma((ncol, OCHUNKS)),
             ) if short else None,
         ],
         compiler_params=pltpu.CompilerParams(
-            collective_id=0, has_side_effects=True, vmem_limit_bytes=60 * 1024 * 1024
+            collective_id=0, has_side_effects=True, vmem_limit_bytes=(40 if short else 60) * 1024 * 1024
         ),
-    )(anc_inverse, panel, diag_inverse, widths, pattern)
+    )(anc_inverse, panel, widths, pattern)
+    strip = pl.BlockSpec((TM, width), lambda j, h: (j * parts + h, 0))
+    square_strip = pl.BlockSpec((TM, SW), lambda j, h: (j * parts + h, 0))
+    return pl.pallas_call(
+        functools.partial(write_out, ncol, parts),
+        grid=(slots, parts),
+        out_shape=(jax.ShapeDtypeStruct((rows, width), F32), jax.ShapeDtypeStruct((rows, SW), F32)),
+        in_specs=[strip, pl.BlockSpec((1, packed, B), lambda j, h: (j, 0, 0)), square_strip, scalar, scalar],
+        out_specs=(strip, square_strip),
+        compiler_params=pltpu.CompilerParams(vmem_limit_bytes=16 * 1024 * 1024),
+    )(product, summed, diag_inverse, widths, pattern)
 
 
 def solution(mesh):

time: 102 us -> 107 us (1.049)
  the two profiles are of different devices: /device:TPU:30 before, /device:TPU:0 now
where the time goes in v2:
time: 107 us
  Pallas kernels  102 us (95%)
  local copies, waits for them, and re-layouts  3.98 us (4%)
    pallas_call x1, Pallas kernels, local(): pl.pallas_call(functools.partial(kernel, sizes), out_shape=(jax.ShapeDtyp...  98.4 us
    unnamed x10, local copies, waits for them, and re-layouts  3.98 us
    pallas_call x1, Pallas kernels, local(): pl.pallas_call(functools.partial(write_out, ncol, parts), grid=(slots, pa...  3.51 us

profile of v2, /device:TPU:0, one launch (start us, length us, event | category | flops | bytes accessed | tf_op | source)
XLA Modules:
  0.0 106.5 jit_solution(3266192449944402771)
XLA Ops:
  0.6 0.0 copy-start
  0.6 1.6 %copy-done = f32[1024,512]{1,0:T(8,128)S(1)} copy-done((f32[1024,512]{1,0:T(8,128)S(1)}, f32[1024,512]{1,0:T(8,128)}, u32[]{:S(2)}) %copy-start) | copy-done | bytes 2097176
  2.2 0.0 copy-start.2
  2.2 1.0 copy-done.2
  3.3 0.0 copy-start.3
  3.3 0.7 copy-done.3
  4.0 0.0 copy-start.4
  4.0 0.7 copy-done.4
  4.6 0.0 copy-start.1
  4.6 98.4 %shard_map.68 = (f32[1024,512]{1,0:T(8,128)S(1)}, f32[2,1056,128]{2,1,0:T(8,128)S(1)}) custom-call(f32[512,256]{1,0:T(8,128)S(1)} %copy-done.2, f32[1024,512]{1,0:T(8,128)S(1)} %copy-done, s32[16]{0:T(128)S(1)} %copy-done.4, s32[16,16]{1,0:T(8,128)S(1)} %copy-done.3), custom_call_target="tpu_custom_call" | custom-call | tf_op jit(solution)/shard_map/pallas_call | solution.py:650
  103.0 0.0 copy-done.1
  103.0 3.5 %shard_map.69 = (f32[1024,512]{1,0:T(8,128)}, f32[1024,512]{1,0:T(8,128)}) custom-call(f32[1024,512]{1,0:T(8,128)S(1)} %get-tuple-element.4.prod_ref, f32[2,1056,128]{2,1,0:T(8,128)S(1)} %get-tuple-element.5.sum_ref, f32[1024,512]{1,0:T(8,128)S(1)} %copy-done.1, s32[16]{0:T(128)S(1)} %copy-done.4, s32[16,16]{1,0:T(8,128)S(1)} %copy-done.3), custom_call_target="tpu_custom_call" | custom-call | tf_op jit(solution)/shard_map/pallas_call | solution.py:691
Async XLA Ops:
  0.6 1.6 %copy-start = (f32[1024,512]{1,0:T(8,128)S(1)}, f32[1024,512]{1,0:T(8,128)}, u32[]{:S(2)}) copy-start(f32[1024,512]{1,0:T(8,128)} %panel_ref.1) | copy-start | bytes 6291460
  2.2 1.0 copy-start.2
  3.3 0.7 copy-start.3
  4.0 0.7 copy-start.4
  4.6 98.4 %copy-start.1 = (f32[1024,512]{1,0:T(8,128)S(1)}, f32[1024,512]{1,0:T(8,128)}, u32[]{:S(2)}) copy-start(f32[1024,512]{1,0:T(8,128)} %diag_ref.1) | copy-start | bytes 6291460

commit v3 on v2

--- a/solution.py
+++ b/solution.py
@@ -70,7 +70,7 @@
     sizes,
     anc_ref, panel_ref, widths_ref, pattern_ref, prod_ref, sum_ref,
     anc, ah, al, ph, plo, pin, opp, oh, ol, qsend, qrecv, upack, urecv, usum, urecv2, ufin,
-    zs, zr, ps, pr, os_, or_, qs, qr, us, ur, us2, ur2, gs2, gr2, gs, gr, crossed,
+    zs, zr, ps, pr, os_, or_, qs, qr, us, ur, us2, ur2, gs2, gr2, gs, gr, anc_own, panel_own, fills, fits, ds, crossed,
 ):
     nsec, nrow, ncol, nf, ns, nb, square = sizes
     rows, width = panel_ref.shape
@@ -97,15 +97,23 @@
             src_ref=src, dst_ref=dst, send_sem=send, recv_sem=recv, device_id=where, device_id_type=MESH
         )
 
+    loads = [
+        pltpu.make_async_copy(source, target, ds.at[i])
+        for i, (source, target) in enumerate(
+            ((widths_ref, fills), (pattern_ref, fits), (anc_ref, anc_own), (panel_ref, panel_own))
+        )
+    ]
+    for one in loads:
+        one.start()
+
     first = (sec * ncol + col) * slots
     blocks = width // B
-    fill = [widths_ref[first + j] for j in range(slots)]
 
     def inside(j, i):
-        return jnp.where(fill[j] > i, 1.0, 0.0).astype(F32)
+        return jnp.where(fills[first + j] > i, 1.0, 0.0).astype(F32)
 
     def present(j, r, c):
-        return pattern_ref[first + j, r * blocks + c].astype(F32)
+        return fits[first + j, r * blocks + c].astype(F32)
 
     def keep(src, j, h, slot, r):
         for i in range(h * wb // parts, (h + 1) * wb // parts):
@@ -187,10 +195,12 @@
                     panel_copy(d, j, h).start()
 
     def settle_own():
-        halves(anc_ref, mine)
+        for one in loads:
+            one.wait()
+        halves(anc_own, mine)
         for j in range(slots):
             for h in range(parts):
-                keep(lambda i, cols: panel_ref[pl.ds(j * SW + i * B, B), cols], j, h, 0, row)
+                keep(lambda i, cols: panel_own[pl.ds(j * SW + i * B, B), cols], j, h, 0, row)
 
     def relay(p, way, c, onward):
         piece_copy(anc_ref, p, way).copies[c].wait_recv()
@@ -406,10 +416,12 @@
         for z in range(ncol):
             pl.when(z != last)(functools.partial(place, z))
         products(1 - spot(last), True)
+        late_step(1, False)
+        late_step(2, True)
         early_step(ncol - 1, 0)
         place(last)
         products(spot(last), False)
-        late_step(1, False)
+        late_step(2, False)
     else:
         for k in range(per):
             products(k, k == 0)
@@ -428,10 +440,10 @@
     lax.fori_loop(0, rows // tm, near, 0)
     if crossed is not None:
         pl.when(late(other))(lambda: late_partner(other))
-        late_partners(1)
-        for t in range(2, ncol):
-            late_step(t, True)
-            late_step(t, False)
+        for t in range(1, ncol):
+            if t > 2:
+                late_step(t, True)
+                late_step(t, False)
             late_partners(t)
     else:
         gather(1)
@@ -538,10 +550,10 @@
         sum_ref[j] = ufin[j]
 
     stages = [update_out, second, third, fourth]
-    for step in range(2 * (slots - 1) + len(stages)):
-        for j in range(slots):
-            if 0 <= step - 2 * j < len(stages):
-                stages[step - 2 * j](j)
+    for step in range(slots - 1 + len(stages)):
+        for j in reversed(range(slots)):
+            if 0 <= step - j < len(stages):
+                stages[step - j](j)
     for j in range(slots):
         finish(j)
 
@@ -647,10 +659,11 @@
     dma = pltpu.SemaphoreType.DMA
     whole = pl.BlockSpec(memory_space=pltpu.VMEM)
     scalar = pl.BlockSpec(memory_space=pltpu.SMEM)
+    far = pl.BlockSpec(memory_space=pltpu.HBM)
     product, summed = pl.pallas_call(
         functools.partial(kernel, sizes),
         out_shape=(jax.ShapeDtypeStruct((rows, width), F32), jax.ShapeDtypeStruct((slots, packed, B), F32)),
-        in_specs=[whole, whole, scalar, scalar],
+        in_specs=[far, far, far, far],
         out_specs=(whole, whole),
         scratch_shapes=[
             vm((pieces, width, pw), F32),
@@ -677,13 +690,15 @@
             dma((slots, nf - 1)), dma((slots, nf - 1)),
             dma((slots, nf - 1)), dma((slots, nf - 1)),
             dma((slots, ns - 1)), dma((slots, ns - 1)),
+            vm((width, pw), F32), vm((rows, width), F32),
+            pltpu.SMEM(widths.shape, widths.dtype), pltpu.SMEM(pattern.shape, pattern.dtype), dma((4,)),
             (
                 vm((ncol, width // 2, pw), F32), dma((2, OCHUNKS)), dma((OCHUNKS,)),
                 dma((ncol, 3, OCHUNKS)), dma((ncol, OCHUNKS)),
             ) if short else None,
         ],
         compiler_params=pltpu.CompilerParams(
-            collective_id=0, has_side_effects=True, vmem_limit_bytes=(40 if short else 60) * 1024 * 1024
+            collective_id=0, has_side_effects=True, vmem_limit_bytes=(49 if short else 60) * 1024 * 1024
         ),
     )(anc_inverse, panel, widths, pattern)
     strip = pl.BlockSpec((TM, width), lambda j, h: (j * parts + h, 0))

time: 107 us -> 92 us (0.86)
  Pallas kernels: 102 us -> 88.6 us
  local copies, waits for them, and re-layouts: 3.98 us -> 2.54 us
    pallas_call x1, Pallas kernels: 98.4 us -> 85.1 us  [local(): pl.pallas_call(functools.partial(kernel, sizes), out_shape=(jax.ShapeDtyp...]
    unnamed x10 -> x8, local copies, waits for them, and re-layouts: 3.98 us -> 2.54 us
where the time goes in v3:
time: 92 us; the launch traced here: 91.8 us
  Pallas kernels  88.6 us (96%)
  local copies, waits for them, and re-layouts  2.54 us (3%)
    pallas_call x1, Pallas kernels, local(): pl.pallas_call(functools.partial(kernel, sizes), out_shape=(jax.ShapeDtyp...  85.1 us
    pallas_call x1, Pallas kernels, local(): pl.pallas_call(functools.partial(write_out, ncol, parts), grid=(slots, pa...  3.51 us
    unnamed x8, local copies, waits for them, and re-layouts  2.54 us

profile of v3, /device:TPU:0, one launch (start us, length us, event | category | flops | bytes accessed | tf_op | source)
XLA Modules:
  0.0 91.8 jit_solution(8531716480912226381)
XLA Ops:
  0.6 0.0 copy-start
  0.6 0.0 copy-start.1
  0.7 1.2 %copy-done.1 = f32[512,256]{1,0:T(8,128)S(1)} copy-done((f32[512,256]{1,0:T(8,128)S(1)}, f32[512,256]{1,0:T(8,128)}, u32[]{:S(2)}) %copy-start.1) | copy-done | bytes 524312
  1.8 0.0 copy-start.2
  1.8 0.7 copy-done.2
  2.5 0.0 copy-start.3
  2.5 0.7 copy-done.3
  3.2 85.1 %shard_map.68 = (f32[1024,512]{1,0:T(8,128)S(1)}, f32[2,1056,128]{2,1,0:T(8,128)S(1)}) custom-call(f32[512,256]{1,0:T(8,128)S(1)} %copy-done.1, f32[1024,512]{1,0:T(8,128)} %panel_ref.1, s32[16]{0:T(128)S(1)} %copy-done.3, s32[16,16]{1,0:T(8,128)S(1)} %copy-done.2), custom_call_target="tpu_custom_call" | custom-call | tf_op jit(solution)/shard_map/pallas_call | solution.py:663
  88.3 0.0 copy-done
  88.3 3.5 %shard_map.69 = (f32[1024,512]{1,0:T(8,128)}, f32[1024,512]{1,0:T(8,128)}) custom-call(f32[1024,512]{1,0:T(8,128)S(1)} %get-tuple-element.4.prod_ref, f32[2,1056,128]{2,1,0:T(8,128)S(1)} %get-tuple-element.5.sum_ref, f32[1024,512]{1,0:T(8,128)S(1)} %copy-done, s32[16]{0:T(128)S(1)} %copy-done.3, s32[16,16]{1,0:T(8,128)S(1)} %copy-done.2), custom_call_target="tpu_custom_call" | custom-call | tf_op jit(solution)/shard_map/pallas_call | solution.py:706
Async XLA Ops:
  0.6 87.7 %copy-start = (f32[1024,512]{1,0:T(8,128)S(1)}, f32[1024,512]{1,0:T(8,128)}, u32[]{:S(2)}) copy-start(f32[1024,512]{1,0:T(8,128)} %diag_ref.1) | copy-start | bytes 6291460
  0.6 1.2 %copy-start.1 = (f32[512,256]{1,0:T(8,128)S(1)}, f32[512,256]{1,0:T(8,128)}, u32[]{:S(2)}) copy-start(f32[512,256]{1,0:T(8,128)} %anc_ref.1) | copy-start | bytes 1572868
  1.8 0.7 copy-start.2
  2.5 0.7 copy-start.3

commit v4 on v3

--- a/solution.py
+++ b/solution.py
@@ -313,10 +313,10 @@
             piece_copy(anc_ref, p, 2).wait_recv()
             halves(anc.at[p], p)
 
-        def late_step(t, ends):
+        def late_step(t, ends, here):
             def wanted(p, z):
                 edge = jnp.logical_or(z == 0, z == ncol - 1)
-                return jnp.logical_and(late(p), edge if ends else jnp.logical_not(edge))
+                return jnp.logical_and(jnp.logical_and(late(p), here), edge if ends else jnp.logical_not(edge))
 
             left = jnp.logical_and(col - t >= 0, wanted(mine - t, col - t))
             right = jnp.logical_and(col + t < ncol, wanted(mine + t, col + t))
@@ -391,10 +391,12 @@
             {"row": at(f, (s + e) % ns)},
         )
 
-    def products(k, fresh):
+    def products(k, fresh, pause=None):
         for j in range(slots):
             for h in range(parts):
                 rr = pl.ds(j * SW + h * tm, tm)
+                if pause is not None and (j + 1) * (h + 1) == slots * parts:
+                    pause()
                 for d in range(1, nf):
                     if fresh:
                         panel_copy(d, j, h).wait_recv()
@@ -412,16 +414,19 @@
         pl.when(early(1 - sec, col))(lambda: from_partner(col))
         lax.fori_loop(1, ncol - 1, early_step, 0)
         pl.when(jnp.logical_and(late(mine), jnp.logical_not(at_end)))(send_mine)
-        late_step(1, True)
+        middle = jnp.logical_not(at_end)
+
+        def forward_late():
+            late_step(1, False, middle)
+            late_step(2, True, middle)
+
+        late_step(1, True, middle)
         for z in range(ncol):
             pl.when(z != last)(functools.partial(place, z))
-        products(1 - spot(last), True)
-        late_step(1, False)
-        late_step(2, True)
+        products(1 - spot(last), True, forward_late)
         early_step(ncol - 1, 0)
         place(last)
         products(spot(last), False)
-        late_step(2, False)
     else:
         for k in range(per):
             products(k, k == 0)
@@ -440,11 +445,12 @@
     lax.fori_loop(0, rows // tm, near, 0)
     if crossed is not None:
         pl.when(late(other))(lambda: late_partner(other))
-        for t in range(1, ncol):
-            if t > 2:
-                late_step(t, True)
-                late_step(t, False)
-            late_partners(t)
+        late_step(1, False, at_end)
+        late_partners(1)
+        late_step(2, False, at_end)
+        late_partners(2)
+        late_step(ncol - 1, True, at_end)
+        late_partners(ncol - 1)
     else:
         gather(1)
 
@@ -518,7 +524,15 @@
         for d in range(1, ns):
             u_copy(j, d).start()
 
+    def negate(j):
+        for i in range(wb):
+            here = pl.ds(j * SW + i * B, B)
+            for c in range(blocks):
+                cols = pl.ds(c * B, B)
+                prod_ref[here, cols] = prod_ref[here, cols] * -(inside(j, i) * present(j, row, c))
+
     def second(j):
+        negate(j)
         for d in range(1, ns):
             u_copy(j, d).wait_recv()
         total = upack[j, portion(s)]
@@ -548,6 +562,8 @@
         for d in range(1, ns):
             g_copy(j, d).wait_recv()
         sum_ref[j] = ufin[j]
+        for i in range(wb):
+            sum_ref[j, pl.ds(tail + 8 + i, 1)] = jnp.broadcast_to(inside(j, i), (1, B))
 
     stages = [update_out, second, third, fourth]
     for step in range(slots - 1 + len(stages)):
@@ -603,27 +619,17 @@
             cross_copies(1).wait_send()
 
 
-def write_out(ncol, parts, prod_ref, sum_ref, diag_ref, widths_ref, pattern_ref, off_ref, upd_ref):
-    j, h = pl.program_id(0), pl.program_id(1)
-    sec, row, col = lax.axis_index("sec"), lax.axis_index("row"), lax.axis_index("col")
-    child = (sec * ncol + col) * pl.num_programs(0) + j
+def write_out(parts, prod_ref, sum_ref, diag_ref, off_ref, upd_ref):
+    h = pl.program_id(1)
     wb = SW // B
     each = wb // parts
-    blocks = off_ref.shape[1] // B
     offs, tail = spots(wb)
     ri = lax.broadcasted_iota(jnp.int32, (B, B), 0)
     ci = lax.broadcasted_iota(jnp.int32, (B, B), 1)
-    fill = widths_ref[child]
+    off_ref[...] = prod_ref[...]
 
     def inside(i):
-        return jnp.where(fill > i, 1.0, 0.0).astype(F32)
-
-    for i in range(each):
-        here = pl.ds(i * B, B)
-        for c in range(blocks):
-            cols = pl.ds(c * B, B)
-            present = pattern_ref[child, row * blocks + c].astype(F32)
-            off_ref[here, cols] = prod_ref[here, cols] * -(inside(h * each + i) * present)
+        return sum_ref[0, pl.ds(tail + 8 + i, 1)]
 
     def block_of(i, k):
         if i < k:
@@ -658,7 +664,6 @@
     vm = pltpu.VMEM
     dma = pltpu.SemaphoreType.DMA
     whole = pl.BlockSpec(memory_space=pltpu.VMEM)
-    scalar = pl.BlockSpec(memory_space=pltpu.SMEM)
     far = pl.BlockSpec(memory_space=pltpu.HBM)
     product, summed = pl.pallas_call(
         functools.partial(kernel, sizes),
@@ -704,13 +709,13 @@
     strip = pl.BlockSpec((TM, width), lambda j, h: (j * parts + h, 0))
     square_strip = pl.BlockSpec((TM, SW), lambda j, h: (j * parts + h, 0))
     return pl.pallas_call(
-        functools.partial(write_out, ncol, parts),
+        functools.partial(write_out, parts),
         grid=(slots, parts),
         out_shape=(jax.ShapeDtypeStruct((rows, width), F32), jax.ShapeDtypeStruct((rows, SW), F32)),
-        in_specs=[strip, pl.BlockSpec((1, packed, B), lambda j, h: (j, 0, 0)), square_strip, scalar, scalar],
+        in_specs=[strip, pl.BlockSpec((1, packed, B), lambda j, h: (j, 0, 0)), square_strip],
         out_specs=(strip, square_strip),
         compiler_params=pltpu.CompilerParams(vmem_limit_bytes=16 * 1024 * 1024),
-    )(product, summed, diag_inverse, widths, pattern)
+    )(product, summed, diag_inverse)
 
 
 def solution(mesh):

time: 92 us -> 87 us (0.946)
  Pallas kernels: 88.6 us -> 83.6 us
    pallas_call x1, Pallas kernels: 85.1 us -> 80.9 us  [local(): pl.pallas_call(functools.partial(kernel, sizes), out_shape=(jax.ShapeDtyp...]
where the time goes in v4:
time: 87 us; the launch traced here: 86.8 us
  Pallas kernels  83.6 us (96%)
  local copies, waits for them, and re-layouts  2.54 us (3%)
    pallas_call x1, Pallas kernels, local(): pl.pallas_call(functools.partial(kernel, sizes), out_shape=(jax.ShapeDtyp...  80.9 us
    pallas_call x1, Pallas kernels, local(): pl.pallas_call(functools.partial(write_out, parts), grid=(slots, parts),...  2.74 us
    unnamed x8, local copies, waits for them, and re-layouts  2.54 us

profile of v4, /device:TPU:0, one launch (start us, length us, event | category | flops | bytes accessed | tf_op | source)
XLA Modules:
  0.0 86.8 jit_solution(14966376383411229443)
XLA Ops:
  0.6 0.0 copy-start
  0.6 0.0 copy-start.1
  0.7 1.2 %copy-done.1 = f32[512,256]{1,0:T(8,128)S(1)} copy-done((f32[512,256]{1,0:T(8,128)S(1)}, f32[512,256]{1,0:T(8,128)}, u32[]{:S(2)}) %copy-start.1) | copy-done | bytes 524312
  1.8 0.0 copy-start.2
  1.8 0.7 copy-done.2
  2.5 0.0 copy-start.3
  2.5 0.7 copy-done.3
  3.2 80.9 %shard_map.68 = (f32[1024,512]{1,0:T(8,128)S(1)}, f32[2,1056,128]{2,1,0:T(8,128)S(1)}) custom-call(f32[512,256]{1,0:T(8,128)S(1)} %copy-done.1, f32[1024,512]{1,0:T(8,128)} %panel_ref.1, s32[16]{0:T(128)S(1)} %copy-done.3, s32[16,16]{1,0:T(8,128)S(1)} %copy-done.2), custom_call_target="tpu_custom_call" | custom-call | tf_op jit(solution)/shard_map/pallas_call | solution.py:668
  84.0 0.0 copy-done
  84.1 2.7 %shard_map.69 = (f32[1024,512]{1,0:T(8,128)}, f32[1024,512]{1,0:T(8,128)}) custom-call(f32[1024,512]{1,0:T(8,128)S(1)} %get-tuple-element.4.prod_ref, f32[2,1056,128]{2,1,0:T(8,128)S(1)} %get-tuple-element.5.sum_ref, f32[1024,512]{1,0:T(8,128)S(1)} %copy-done), custom_call_target="tpu_custom_call" | custom-call | tf_op jit(solution)/shard_map/pallas_call | solution.py:711
Async XLA Ops:
  0.6 83.4 %copy-start = (f32[1024,512]{1,0:T(8,128)S(1)}, f32[1024,512]{1,0:T(8,128)}, u32[]{:S(2)}) copy-start(f32[1024,512]{1,0:T(8,128)} %diag_ref.1) | copy-start | bytes 6291460
  0.6 1.2 %copy-start.1 = (f32[512,256]{1,0:T(8,128)S(1)}, f32[512,256]{1,0:T(8,128)}, u32[]{:S(2)}) copy-start(f32[512,256]{1,0:T(8,128)} %anc_ref.1) | copy-start | bytes 1572868
  1.8 0.7 copy-start.2
  2.5 0.7 copy-start.3

commit v5 on v4

--- a/solution.py
+++ b/solution.py
@@ -705,7 +705,7 @@
         compiler_params=pltpu.CompilerParams(
             collective_id=0, has_side_effects=True, vmem_limit_bytes=(49 if short else 60) * 1024 * 1024
         ),
-    )(anc_inverse, panel, widths, pattern)
+    )(*(pltpu.with_memory_space_constraint(x, pltpu.HBM) for x in (anc_inverse, panel, widths, pattern)))
     strip = pl.BlockSpec((TM, width), lambda j, h: (j * parts + h, 0))
     square_strip = pl.BlockSpec((TM, SW), lambda j, h: (j * parts + h, 0))
     return pl.pallas_call(

time: 87 us -> 84.8 us (0.975)
  local copies, waits for them, and re-layouts: 2.54 us -> 0.01 us
    unnamed x8 -> x2, local copies, waits for them, and re-layouts: 2.54 us -> 0.01 us
where the time goes in v5:
time: 84.8 us; the launch traced here: 84.6 us
  Pallas kernels  84 us (99%)
    pallas_call x1, Pallas kernels, local(): pl.pallas_call(functools.partial(kernel, sizes), out_shape=(jax.ShapeDtyp...  81.2 us
    pallas_call x1, Pallas kernels, local(): pl.pallas_call(functools.partial(write_out, parts), grid=(slots, parts),...  2.74 us

profile of v5, /device:TPU:0, one launch (start us, length us, event | category | flops | bytes accessed | tf_op | source)
XLA Modules:
  0.0 84.6 jit_solution(15602301757004914780)
XLA Ops:
  0.6 0.0 copy-start
  0.6 81.2 %shard_map.68 = (f32[1024,512]{1,0:T(8,128)S(1)}, f32[2,1056,128]{2,1,0:T(8,128)S(1)}) custom-call(f32[512,256]{1,0:T(8,128)} %anc_ref.1, f32[1024,512]{1,0:T(8,128)} %panel_ref.1, s32[16]{0:T(128)} %widths_ref.1, s32[16,16]{1,0:T(8,128)} %pattern_ref.1), custom_call_target="tpu_custom_call" | custom-call | tf_op jit(solution)/shard_map/pallas_call | solution.py:668
  81.9 0.0 copy-done
  81.9 2.7 %shard_map.69 = (f32[1024,512]{1,0:T(8,128)}, f32[1024,512]{1,0:T(8,128)}) custom-call(f32[1024,512]{1,0:T(8,128)S(1)} %get-tuple-element.4.prod_ref, f32[2,1056,128]{2,1,0:T(8,128)S(1)} %get-tuple-element.5.sum_ref, f32[1024,512]{1,0:T(8,128)S(1)} %copy-done), custom_call_target="tpu_custom_call" | custom-call | tf_op jit(solution)/shard_map/pallas_call | solution.py:711
Async XLA Ops:
  0.6 81.2 %copy-start = (f32[1024,512]{1,0:T(8,128)S(1)}, f32[1024,512]{1,0:T(8,128)}, u32[]{:S(2)}) copy-start(f32[1024,512]{1,0:T(8,128)} %diag_ref.1) | copy-start | bytes 6291460
